TPU v7x, 128 devices: a whole 4x4x4 slice. The times are simulated.
128 devices in a mesh: expert: 64 (over x, y, z), dp: 2 (over core).
Axes of the slice: x: 4, y: 4, z: 4, core: 2. Of those that a mesh axis runs over, the one named last changes fastest.
Arguments:
- tokens: bfloat16 [12288, 4096], P(('expert', 'dp')), may hold values from -6 to 6
- w_gate: bfloat16 [128, 4096, 768], P(('expert', 'dp')), may hold values from -0.09375 to 0.09375
- w_up: bfloat16 [128, 4096, 768], P(('expert', 'dp')), may hold values from -0.09375 to 0.09375
- w_down: bfloat16 [128, 768, 4096], P(('expert', 'dp')), may hold values from -0.21875 to 0.21875
- route_ids: int32 [12288, 8], P(('expert', 'dp')), may hold values from 0 to 127, all different within a row
- route_gates: float32 [12288, 8], P(('expert', 'dp')), may hold values from 0.05 to 0.4
- hot_experts: int32 [1], replicated, may hold values from 0 to 127
Outputs:
- mixed: bfloat16 [12288, 4096], P(('expert', 'dp'))
Inputs may be any that keep to these rules, and one draw needn't show every extreme that they name: `route_ids`: each row names 8 different experts.
All inputs are finite; a program needn't handle non-finite values.
Results may differ from a plain program's by a relative error of at most 0.007.
Values may be sent and summed in bfloat16 or wider, within the bound.
A program may use at most 192 MiB of HBM per device.

v0:
```python
import jax
import jax.numpy as jnp
from jax import lax
from jax.sharding import PartitionSpec as P

CAP = 6


def expert_ffn(in_rows, gate_w, up_w, down_w):
    gate_val = jnp.dot(in_rows, gate_w, preferred_element_type=jnp.float32)
    up_val = jnp.dot(in_rows, up_w, preferred_element_type=jnp.float32)
    hidden = (jax.nn.silu(gate_val) * up_val).astype(jnp.bfloat16)
    return jnp.dot(hidden, down_w, preferred_element_type=jnp.float32).astype(jnp.bfloat16)


def on_device(tokens, w_gate, w_up, w_down, route_ids, route_gates, hot_experts):
    feat_width = tokens.shape[1]
    tok_rows = tokens.shape[0]
    top_k = route_ids.shape[1]
    n_dp = lax.axis_size("dp")
    experts = lax.axis_size("expert") * n_dp
    hot_id = hot_experts[0]
    me = lax.axis_index("expert") * n_dp + lax.axis_index("dp")
    own = (w_gate[0], w_up[0], w_down[0])
    with jax.named_scope("hot_weight_broadcast"):
        is_root = me == hot_id
        hot_w = tuple(
            (lax.psum(jnp.where(is_root, w, jnp.zeros_like(w)), ("expert", "dp")) for w in own)
        )
    with jax.named_scope("routing"):
        flat_ids = route_ids.reshape(-1)
        labels = lax.iota(jnp.int32, experts)
        onehot = (flat_ids[:, None] == labels[None, :]).astype(jnp.int32)
        rank_of = jnp.sum(onehot * (jnp.cumsum(onehot, axis=0) - 1), axis=1)
        is_kept = (flat_ids != hot_id) & (rank_of < CAP)
        slot_of = jnp.where(is_kept, flat_ids * CAP + rank_of, experts * CAP)
        slots = lax.iota(jnp.int32, experts * CAP)
        hit = slot_of[None, :] == slots[:, None]
        dispatch = jnp.any(hit.reshape(experts * CAP, tok_rows, top_k), axis=2)
    with jax.named_scope("dispatch"):
        outgoing = jnp.dot(
            dispatch.astype(tokens.dtype), tokens, preferred_element_type=jnp.float32
        ).astype(tokens.dtype)
        to_send = outgoing.reshape(experts, CAP * feat_width)
        arrived = lax.all_to_all(to_send, ("expert", "dp"), 0, 0, tiled=True)
    with jax.named_scope("expert_ffn"):
        results = expert_ffn(arrived.reshape(-1, feat_width), *own)
    with jax.named_scope("return"):
        come_back = lax.all_to_all(
            results.reshape(experts, CAP * feat_width), ("expert", "dp"), 0, 0, tiled=True
        )
        returned = come_back.reshape(experts * CAP, feat_width)
    with jax.named_scope("combine"):
        gate_flat = route_gates.reshape(-1)
        cold_weight = jnp.where(is_kept, gate_flat, jnp.zeros_like(gate_flat))
        weight_of_slot = jnp.where(hit, cold_weight[None, :], 0.0)
        combine = jnp.sum(weight_of_slot.reshape(experts * CAP, tok_rows, top_k), axis=2).T
        cold_sum = jnp.dot(
            combine,
            returned.astype(jnp.float32),
            precision=lax.Precision.HIGHEST,
            preferred_element_type=jnp.float32,
        )
    with jax.named_scope("hot_expert"):
        hot_out = expert_ffn(tokens, *hot_w)
        hot_weight = jnp.sum(
            jnp.where(route_ids == hot_id, route_gates, jnp.zeros_like(route_gates)), axis=1
        )
        combined = cold_sum + hot_weight[:, None] * hot_out.astype(jnp.float32)
    return combined.astype(jnp.bfloat16)


def solution(mesh):
    in_specs = (
        P(("expert", "dp"), None),
        P(("expert", "dp"), None, None),
        P(("expert", "dp"), None, None),
        P(("expert", "dp"), None, None),
        P(("expert", "dp"), None),
        P(("expert", "dp"), None),
        P(),
    )
    out_specs = P(("expert", "dp"), None)
    return jax.shard_map(
        on_device, mesh=mesh, in_specs=in_specs, out_specs=out_specs, check_vma=False
    )
```

profile of v0, /device:TPU:0, one launch (start us, length us, event | category | flops | bytes accessed | tf_op | source)
XLA Modules:
  0.0 559.9 jit_solution(3620452224844530923)
XLA Ops:
  6.5 0.0 copy-start
  6.5 0.9 copy.64
  7.4 0.1 eq.51
  7.5 0.1 eq.47
  8.2 0.1 copy.66
  8.3 0.2 fusion.13
  8.6 0.1 add_add_fusion
  8.6 0.1 copy.67
  8.7 0.3 fusion.15
  9.0 0.1 reduce_sum.30
  9.1 0.1 copy.68
  9.2 0.7 add_select_fusion
  9.9 0.1 copy.70
  10.0 0.8 fusion.8
  10.8 4.5 convolution_convert_fusion
  15.2 23.8 %all_to_all.16 = bf16[128,1,24576]{2,1,0:T(2,128)(2,1)} reshape(bf16[768,4096]{1,0:T(8,128)(2,1)} %convolution_convert_fusion) | data formatting | bytes 12582912 | tf_op jit(solution)/shard_map/dispatch/all_to_all | solution.py:45
  39.0 0.5 broadcast.85
  39.4 38.9 %reduce.2 = bf16[128,24576]{1,0:T(8,128)(2,1)} reduce(bf16[128,1,24576]{2,1,0:T(2,128)(2,1)} %all_to_all.16, bf16[]{:T(256)} %broadcast.85), dimensions={1}, to_apply=%all_to_all.16.reduce_sub_computation | reduce | bytes 12582914 | tf_op jit(solution)/shard_map/dispatch/all_to_all | solution.py:45
  78.3 9.4 %reshape.90 = bf16[128,2,12288]{2,1,0:T(2,128)(2,1)} reshape(bf16[128,24576]{1,0:T(8,128)(2,1)} %reduce.2) | data formatting | bytes 12582912
  87.7 11.6 %all-to-all-start = ((bf16[128,2,12288]{2,1,0:T(2,128)(2,1)}), bf16[128,2,12288]{2,1,0:T(2,128)(2,1)}, u32[]{:S(2)}, u32[]{:S(2)}) async-start(bf16[128,2,12288]{2,1,0:T(2,128)(2,1)} %reshape.90), calls=%async_computation | async-start | bytes 12582912 | tf_op jit(solution)/shard_map/dispatch/all_to_all | solution.py:45
  99.3 0.0 all-reduce.3.cloned.1.call-start
  99.4 5.9 %bitcast_select_fusion = bf16[768,4096]{1,0:T(8,128)(2,1)} fusion(bf16[1,768,4096]{2,1,0:T(8,128)(2,1)} %param.10, pred[]{:T(512)S(6)} %eq.59), kind=kLoop, calls=%fused_computation.2 | loop fusion | flops 3145728 | bytes 12582913 | tf_op jit(solution)/shard_map/hot_weight_broadcast/jit(_where)/select_n | solution.py:28
  105.3 9.9 %bitcast_select_fusion.1 = (bf16[4096,768]{1,0:T(8,128)(2,1)}, bf16[4096,768]{1,0:T(8,128)(2,1)}) fusion(bf16[1,4096,768]{2,1,0:T(8,128)(2,1)} %param.9, pred[]{:T(512)S(6)} %eq.59, bf16[1,4096,768]{2,1,0:T(8,128)(2,1)} %param.8), kind=kLoop, calls=%fused_computation.4 | loop fusion | flops 6291456 | bytes 25165824 | tf_op jit(solution)/shard_map/hot_weight_broadcast/jit(_where)/select_n | solution.py:28
  115.1 0.0 all-reduce.3.cloned.1.call-update
  115.1 65.2 %all-to-all-done = bf16[128,2,12288]{2,1,0:T(2,128)(2,1)} async-done(((bf16[128,2,12288]{2,1,0:T(2,128)(2,1)}), bf16[128,2,12288]{2,1,0:T(2,128)(2,1)}, u32[]{:S(2)}, u32[]{:S(2)}) %all-to-all-start) | async-done | bytes 6291488 | tf_op jit(solution)/shard_map/dispatch/all_to_all | solution.py:45
  180.4 34.5 %reshape.91 = bf16[128,1,24576]{2,1,0:T(2,128)(2,1)} reshape(bf16[128,2,12288]{2,1,0:T(2,128)(2,1)} %all-to-all-done) | data formatting | bytes 12582912
  214.8 38.3 %reduce = bf16[128,24576]{1,0:T(8,128)(2,1)} reduce(bf16[128,1,24576]{2,1,0:T(2,128)(2,1)} %reshape.91, bf16[]{:T(256)} %constant.43), dimensions={1}, to_apply=%all_to_all.13.reduce_sub_computation | reduce | bytes 12582914 | tf_op jit(solution)/shard_map/dispatch/all_to_all | solution.py:45
  253.2 11.2 %reshape.86 = bf16[768,4096]{1,0:T(8,128)(2,1)} reshape(bf16[128,24576]{1,0:T(8,128)(2,1)} %reduce) | data formatting | bytes 12582912 | tf_op jit(solution)/shard_map/expert_ffn/reshape | solution.py:47
  264.4 9.1 %fusion.3 = f32[768,768]{1,0:T(8,128)S(1)} fusion(bf16[768,4096]{1,0:T(8,128)(2,1)} %reshape.86, bf16[1,4096,768]{2,1,0:T(8,128)(2,1)} %param.8), kind=kOutput, calls=%fused_computation.8 | convolution fusion | flops 4831838208 | bytes 14942208 | tf_op jit(solution)/shard_map/expert_ffn/dot_general | solution.py:10
  273.5 0.0 copy-done.1
  273.5 8.0 %multiply_convert_fusion = bf16[768,768]{1,0:T(8,128)(2,1)S(1)} fusion(f32[768,768]{1,0:T(8,128)S(1)} %fusion.3, bf16[768,4096]{1,0:T(8,128)(2,1)S(1)} %copy-done.1, bf16[1,4096,768]{2,1,0:T(8,128)(2,1)} %param.9), kind=kOutput, calls=%fused_computation.15 | convolution fusion | flops 4835377152 | bytes 16121856 | tf_op jit(solution)/shard_map/expert_ffn/dot_general | solution.py:11
  281.6 0.0 slice-done
  281.6 0.0 slice-done.1
  281.6 7.1 %convolution_convert_fusion.1 = bf16[768,4096]{1,0:T(8,128)(2,1)} fusion(bf16[768,768]{1,0:T(8,128)(2,1)S(1)} %multiply_convert_fusion, bf16[1,768,4096]{2,1,0:T(8,128)(2,1)S(1)} %bitcast.50), kind=kOutput, calls=%fused_computation.1 | convolution fusion | flops 4834983936 | bytes 13762560 | tf_op jit(solution)/shard_map/expert_ffn/dot_general | solution.py:13
  288.7 23.9 %all_to_all.17 = bf16[128,1,24576]{2,1,0:T(2,128)(2,1)} reshape(bf16[768,4096]{1,0:T(8,128)(2,1)} %convolution_convert_fusion.1) | data formatting | bytes 12582912 | tf_op jit(solution)/shard_map/return/all_to_all | solution.py:49
  312.5 38.8 %reduce.3 = bf16[128,24576]{1,0:T(8,128)(2,1)} reduce(bf16[128,1,24576]{2,1,0:T(2,128)(2,1)} %all_to_all.17, bf16[]{:T(256)} %broadcast.85), dimensions={1}, to_apply=%all_to_all.17.reduce_sub_computation | reduce | bytes 12582914 | tf_op jit(solution)/shard_map/return/all_to_all | solution.py:49
  351.4 9.7 %reshape.92 = bf16[128,2,12288]{2,1,0:T(2,128)(2,1)} reshape(bf16[128,24576]{1,0:T(8,128)(2,1)} %reduce.3) | data formatting | bytes 12582912
  361.1 7.8 %all-to-all-start.1 = ((bf16[128,2,12288]{2,1,0:T(2,128)(2,1)}), bf16[128,2,12288]{2,1,0:T(2,128)(2,1)}, u32[]{:S(2)}, u32[]{:S(2)}) async-start(bf16[128,2,12288]{2,1,0:T(2,128)(2,1)} %reshape.92), calls=%async_computation.1 | async-start | bytes 12582912 | tf_op jit(solution)/shard_map/return/all_to_all | solution.py:49
  368.9 0.1 copy.71
  369.0 0.8 select_reduce_fusion
  369.8 81.9 %all-reduce.3.cloned.1.call-done = (bf16[768,4096]{1,0:T(8,128)(2,1)}, bf16[4096,768]{1,0:T(8,128)(2,1)}, bf16[4096,768]{1,0:T(8,128)(2,1)}) async-done(((bf16[768,4096]{1,0:T(8,128)(2,1)}, bf16[4096,768]{1,0:T(8,128)(2,1)}, bf16[4096,768]{1,0:T(8,128)(2,1)}), (bf16[768,4096]{1,0:T(8,128)(2,1)}, bf16[4096,768]{1,0:T(8,128)(2,1)}, bf16[4096,768]{1,0:T(8,128)(2,1)})) %all-reduce.3.cloned.1.call-update) | async-done | bytes 18874384 | tf_op jit(solution)/shard_map/hot_weight_broadcast/psum | solution.py:28
  451.7 3.9 convolution_bitcast_fusion.1
  455.6 7.1 %fusion.7 = f32[96,4096]{1,0:T(8,128)S(1)} fusion(bf16[768,4096]{1,0:T(8,128)(2,1)} %get-tuple-element.5, bf16[96,4096]{1,0:T(8,128)(2,1)S(1)} %copy-done, bf16[4096,768]{1,0:T(8,128)(2,1)} %get-tuple-element.6, f32[96]{0:T(128)S(1)} %get-tuple-element.9, f32[96,768]{1,0:T(8,128)S(1)} %convolution_bitcast_fusion.1), kind=kOutput, calls=%fused_computation.14 | convolution fusion | flops 1209581568 | bytes 15237504 | tf_op jit(solution)/shard_map/hot_expert/dot_general | solution.py:13
  462.7 0.0 all-to-all-done.1
  462.8 33.8 %reshape.93 = bf16[128,1,24576]{2,1,0:T(2,128)(2,1)} reshape(bf16[128,2,12288]{2,1,0:T(2,128)(2,1)} %all-to-all-done.1) | data formatting | bytes 12582912
  496.6 38.3 %reduce.1 = bf16[128,24576]{1,0:T(8,128)(2,1)} reduce(bf16[128,1,24576]{2,1,0:T(2,128)(2,1)} %reshape.93, bf16[]{:T(256)} %constant.43), dimensions={1}, to_apply=%all_to_all.15.reduce_sub_computation | reduce | bytes 12582914 | tf_op jit(solution)/shard_map/return/all_to_all | solution.py:49
  534.9 11.1 %reshape.87 = bf16[768,4096]{1,0:T(8,128)(2,1)} reshape(bf16[128,24576]{1,0:T(8,128)(2,1)} %reduce.1) | data formatting | bytes 12582912 | tf_op jit(solution)/shard_map/return/reshape | solution.py:52
  546.0 6.8 %fusion.5 = bf16[96,4096]{1,0:T(8,128)(2,1)} fusion(f32[96,4096]{1,0:T(8,128)S(1)} %fusion.7, f32[768,96]{0,1:T(8,128)S(1)} %select_reduce_fusion, bf16[768,4096]{1,0:T(8,128)(2,1)} %reshape.87), kind=kOutput, calls=%fused_computation.11 | convolution fusion | flops 3624665088 | bytes 8945664 | tf_op jit(solution)/shard_map/combine/dot_general | solution.py:58
  (12 shorter events, 0.1 us)
Async XLA Ops:
  6.5 4.2 copy-start
  87.7 92.7 %all-to-all-start = ((bf16[128,2,12288]{2,1,0:T(2,128)(2,1)}), bf16[128,2,12288]{2,1,0:T(2,128)(2,1)}, u32[]{:S(2)}, u32[]{:S(2)}) async-start(bf16[128,2,12288]{2,1,0:T(2,128)(2,1)} %reshape.90), calls=%async_computation | async-start | bytes 12582912 | tf_op jit(solution)/shard_map/dispatch/all_to_all | solution.py:45
  99.3 352.4 %all-reduce.3.cloned.1.call-start = ((), (), s32[]{:S(2)}) async-start(), calls=%async_computation.2 | async-start | bytes 37748736 | tf_op jit(solution)/shard_map/hot_weight_broadcast/psum | solution.py:28
  253.2 28.4 %slice-start = ((s8[6291456]{0:T(1024)(128)(4,1)}), s8[2097152]{0:T(1024)(128)(4,1)S(1)}, s32[]{:S(2)}) async-start(s8[6291456]{0:T(1024)(128)(4,1)} %bitcast.49), calls=%async_computation.3 | async-start | bytes 4194304
  264.4 9.1 %copy-start.1 = (bf16[768,4096]{1,0:T(8,128)(2,1)S(1)}, bf16[768,4096]{1,0:T(8,128)(2,1)}, u32[]{:S(2)}) copy-start(bf16[768,4096]{1,0:T(8,128)(2,1)} %reshape.86) | copy-start | bytes 18874372
  264.4 17.2 %slice-start.1 = ((s8[6291456]{0:T(1024)(128)(4,1)}), s8[4194304]{0:T(1024)(128)(4,1)S(1)}, s32[]{:S(2)}) async-start(s8[6291456]{0:T(1024)(128)(4,1)} %bitcast.49), calls=%async_computation.4 | async-start | bytes 8388608
  361.1 7.8 %copy-start.2 = (s32[96,8]{0,1:T(8,128)S(1)}, s32[96,8]{0,1:T(8,128)}, u32[]{:S(2)}) copy-start(s32[96,8]{0,1:T(8,128)} %param.11) | copy-start | bytes 9220
  361.1 7.8 %copy-start.3 = (f32[96,8]{0,1:T(8,128)S(1)}, f32[96,8]{0,1:T(8,128)}, u32[]{:S(2)}) copy-start(f32[96,8]{0,1:T(8,128)} %param.12) | copy-start | bytes 9220
  361.1 101.7 %all-to-all-start.1 = ((bf16[128,2,12288]{2,1,0:T(2,128)(2,1)}), bf16[128,2,12288]{2,1,0:T(2,128)(2,1)}, u32[]{:S(2)}, u32[]{:S(2)}) async-start(bf16[128,2,12288]{2,1,0:T(2,128)(2,1)} %reshape.92), calls=%async_computation.1 | async-start | bytes 12582912 | tf_op jit(solution)/shard_map/return/all_to_all | solution.py:49
Sparse Core Ops, SparseCore 0:
  115.3 336.3 all-reduce.2
where the time goes:
time: 571 us; the launch traced here: 560 us
  other arithmetic  173 us (30%)
  local copies, waits for them, and re-layouts  159 us (28%)
  waiting for transfers between devices  147 us (26%)
  matrix products  46.5 us (8%)
  starting transfers between devices  19.5 us (3%)
  between operations  14.5 us (3%)
    unnamed x17, local copies, waits for them, and re-layouts  88.2 us
    psum x1, waiting for transfers between devices, on_device(): lax.psum(jnp.where(is_root, w, jnp.zeros_like(w)), ('expert', 'dp'))  81.9 us
    all_to_all x2, other arithmetic, on_device(): arrived = lax.all_to_all(to_send, ('expert', 'dp'), 0, 0, tiled=True)  77.2 us
    all_to_all x2, other arithmetic, on_device(): lax.all_to_all(results.reshape(experts, CAP * feat_width), ('expert', 'dp...  77.2 us
    all_to_all x1, waiting for transfers between devices, on_device(): arrived = lax.all_to_all(to_send, ('expert', 'dp'), 0, 0, tiled=True)  65.2 us
    all_to_all x2, local copies, waits for them, and re-layouts, on_device(): arrived = lax.all_to_all(to_send, ('expert', 'dp'), 0, 0, tiled=True)  24.2 us
    all_to_all x1, local copies, waits for them, and re-layouts, on_device(): lax.all_to_all(results.reshape(experts, CAP * feat_width), ('expert', 'dp...  23.9 us
    select_n x2, other arithmetic, on_device(): jnp.where(is_root, w, jnp.zeros_like(w))  15.8 us
  transfers between devices with their start and end apart: 3, of which 2 were waited for; matrix products, arithmetic and copies ran while one was open for 33% of the time, Pallas kernels for 0%

commit v1 on v0

--- a/solution.py
+++ b/solution.py
@@ -1,9 +1,19 @@
+import functools
 import jax
 import jax.numpy as jnp
 from jax import lax
 from jax.sharding import PartitionSpec as P
 
 CAP = 6
+
+
+def _part_units(array_in, mesh_dim, device_axis):
+    for dev in (mesh_dim, device_axis):
+        array_in = lax.psum(array_in, axis_name=dev)
+    return array_in
+
+
+face_list = functools.partial(_part_units, mesh_dim="dp", device_axis="expert")
 
 
 def expert_ffn(in_rows, gate_w, up_w, down_w):
@@ -24,9 +34,7 @@
     own = (w_gate[0], w_up[0], w_down[0])
     with jax.named_scope("hot_weight_broadcast"):
         is_root = me == hot_id
-        hot_w = tuple(
-            (lax.psum(jnp.where(is_root, w, jnp.zeros_like(w)), ("expert", "dp")) for w in own)
-        )
+        hot_w = tuple((face_list(jnp.where(is_root, w, jnp.zeros_like(w))) for w in own))
     with jax.named_scope("routing"):
         flat_ids = route_ids.reshape(-1)
         labels = lax.iota(jnp.int32, experts)

time: 571 us -> 649 us (1.14)
  blocking collectives: 0 us -> 90 us
  starting transfers between devices: 19.5 us -> 8.54 us
    all_to_all x0 -> x1, blocking collectives: none -> 90 us  [on_device(): arrived = lax.all_to_all(to_send, ('expert', 'dp'), 0, 0, tiled=True)]
    all_to_all x1, waiting for transfers between devices: 0.01 us -> 74.8 us  [on_device(): lax.all_to_all(results.reshape(experts, CAP * feat_width), ('expert', 'dp...]
    all_to_all x1 -> x0, waiting for transfers between devices: 65.2 us -> none  [on_device(): arrived = lax.all_to_all(to_send, ('expert', 'dp'), 0, 0, tiled=True)]
    all_to_all x1 -> x0, starting transfers between devices: 11.6 us -> none  [on_device(): arrived = lax.all_to_all(to_send, ('expert', 'dp'), 0, 0, tiled=True)]
    psum x1 -> x2, waiting for transfers between devices: 81.9 us -> 71.1 us  [_part_units(): array_in = lax.psum(array_in, axis_name=dev)]
  transfers between devices with their start and end apart: 3 -> 3, of which waited for: 2 -> 2; matrix products, arithmetic and copies ran while one was open for 33% -> 46% of each run, Pallas kernels for 0% -> 0%
where the time goes in v1:
time: 649 us; the launch traced here: 637 us
  other arithmetic  172 us (27%)
  local copies, waits for them, and re-layouts  159 us (24%)
  waiting for transfers between devices  146 us (22%)
  blocking collectives  90 us (14%)
  matrix products  46.9 us (7%)
  between operations  14.5 us (2%)
  starting transfers between devices  8.54 us (1%)
    all_to_all x1, blocking collectives, on_device(): arrived = lax.all_to_all(to_send, ('expert', 'dp'), 0, 0, tiled=True)  90 us
    unnamed x17, local copies, waits for them, and re-layouts  87.2 us
    all_to_all x2, other arithmetic, on_device(): arrived = lax.all_to_all(to_send, ('expert', 'dp'), 0, 0, tiled=True)  77.1 us
    all_to_all x2, other arithmetic, on_device(): lax.all_to_all(results.reshape(experts, CAP * feat_width), ('expert', 'dp...  77.1 us
    all_to_all x1, waiting for transfers between devices, on_device(): lax.all_to_all(results.reshape(experts, CAP * feat_width), ('expert', 'dp...  74.8 us
    psum x2, waiting for transfers between devices, _part_units(): array_in = lax.psum(array_in, axis_name=dev)  71.1 us
    all_to_all x2, local copies, waits for them, and re-layouts, on_device(): arrived = lax.all_to_all(to_send, ('expert', 'dp'), 0, 0, tiled=True)  24.4 us
    all_to_all x1, local copies, waits for them, and re-layouts, on_device(): lax.all_to_all(results.reshape(experts, CAP * feat_width), ('expert', 'dp...  24 us
  transfers between devices with their start and end apart: 3, of which 2 were waited for; matrix products, arithmetic and copies ran while one was open for 46% of the time, Pallas kernels for 0%

profile of v1, /device:TPU:0, one launch (start us, length us, event | category | flops | bytes accessed | tf_op | source)
XLA Modules:
  0.0 637.0 jit_solution(18446463856281684283)
XLA Ops:
  6.5 0.0 copy-start
  6.5 0.0 all-reduce.7.cloned.1.call-start
  7.3 5.9 bitcast_select_fusion
  13.1 10.0 %bitcast_select_fusion.1 = (bf16[4096,768]{1,0:T(8,128)(2,1)}, bf16[4096,768]{1,0:T(8,128)(2,1)}) fusion(bf16[1,4096,768]{2,1,0:T(8,128)(2,1)} %param.9, pred[]{:T(512)S(6)} %eq.59, bf16[1,4096,768]{2,1,0:T(8,128)(2,1)} %param.8), kind=kLoop, calls=%fused_computation.4 | loop fusion | flops 6291456 | bytes 25165824 | tf_op jit(solution)/shard_map/hot_weight_broadcast/jit(_where)/select_n | solution.py:37
  23.1 0.0 all-reduce.7.cloned.1.call-update
  23.2 0.0 all-reduce.5.cloned.1.call-start
  23.2 0.6 copy-done.2
  23.8 0.1 copy.64
  23.9 0.1 eq.51
  24.0 0.1 copy.66
  24.1 0.2 fusion.13
  24.4 71.1 %all-reduce.7.cloned.1.call-done = (bf16[768,4096]{1,0:T(8,128)(2,1)}, bf16[4096,768]{1,0:T(8,128)(2,1)}, bf16[4096,768]{1,0:T(8,128)(2,1)}) async-done(((bf16[768,4096]{1,0:T(8,128)(2,1)}, bf16[4096,768]{1,0:T(8,128)(2,1)}, bf16[4096,768]{1,0:T(8,128)(2,1)}), (bf16[768,4096]{1,0:T(8,128)(2,1)}, bf16[4096,768]{1,0:T(8,128)(2,1)}, bf16[4096,768]{1,0:T(8,128)(2,1)})) %all-reduce.7.cloned.1.call-update) | async-done | bytes 18874384 | tf_op jit(solution)/shard_map/hot_weight_broadcast/psum | solution.py:12
  95.4 0.0 all-reduce.5.cloned.1.call-update
  95.5 0.1 eq.47
  95.6 0.1 copy.67
  95.7 0.3 fusion.15
  96.0 0.1 reduce_sum.30
  96.1 0.1 copy.68
  96.1 0.1 copy.70
  96.2 0.8 fusion.8
  97.0 0.0 copy-done
  97.0 4.4 convolution_convert_fusion
  101.5 23.9 %all_to_all.16 = bf16[128,1,24576]{2,1,0:T(2,128)(2,1)} reshape(bf16[768,4096]{1,0:T(8,128)(2,1)} %convolution_convert_fusion) | data formatting | bytes 12582912 | tf_op jit(solution)/shard_map/dispatch/all_to_all | solution.py:53
  125.4 0.5 broadcast.85
  125.8 38.8 %reduce.2 = bf16[128,24576]{1,0:T(8,128)(2,1)} reduce(bf16[128,1,24576]{2,1,0:T(2,128)(2,1)} %all_to_all.16, bf16[]{:T(256)} %broadcast.85), dimensions={1}, to_apply=%all_to_all.16.reduce_sub_computation | reduce | bytes 12582914 | tf_op jit(solution)/shard_map/dispatch/all_to_all | solution.py:53
  164.7 9.5 %reshape.90 = bf16[128,2,12288]{2,1,0:T(2,128)(2,1)} reshape(bf16[128,24576]{1,0:T(8,128)(2,1)} %reduce.2) | data formatting | bytes 12582912
  174.2 90.0 %all_to_all.20 = bf16[128,2,12288]{2,1,0:T(2,128)(2,1)} all-to-all(bf16[128,2,12288]{2,1,0:T(2,128)(2,1)} %reshape.90), channel_id=1, replica_groups=mesh['expert'=64,'dp'=2] {'expert','dp'}, dimensions={0} | all-to-all | bytes 12582912 | tf_op jit(solution)/shard_map/dispatch/all_to_all | solution.py:53
  264.1 33.8 %reshape.91 = bf16[128,1,24576]{2,1,0:T(2,128)(2,1)} reshape(bf16[128,2,12288]{2,1,0:T(2,128)(2,1)} %all_to_all.20) | data formatting | bytes 12582912
  298.0 38.3 %reduce = bf16[128,24576]{1,0:T(8,128)(2,1)} reduce(bf16[128,1,24576]{2,1,0:T(2,128)(2,1)} %reshape.91, bf16[]{:T(256)} %constant.43), dimensions={1}, to_apply=%all_to_all.13.reduce_sub_computation | reduce | bytes 12582914 | tf_op jit(solution)/shard_map/dispatch/all_to_all | solution.py:53
  336.3 11.5 %reshape.86 = bf16[768,4096]{1,0:T(8,128)(2,1)} reshape(bf16[128,24576]{1,0:T(8,128)(2,1)} %reduce) | data formatting | bytes 12582912 | tf_op jit(solution)/shard_map/expert_ffn/reshape | solution.py:55
  347.8 9.4 %fusion.3 = f32[768,768]{1,0:T(8,128)S(1)} fusion(bf16[768,4096]{1,0:T(8,128)(2,1)} %reshape.86, bf16[1,4096,768]{2,1,0:T(8,128)(2,1)} %param.8), kind=kOutput, calls=%fused_computation.8 | convolution fusion | flops 4831838208 | bytes 14942208 | tf_op jit(solution)/shard_map/expert_ffn/dot_general | solution.py:20
  357.2 0.0 copy-done.1
  357.2 8.2 %multiply_convert_fusion = bf16[768,768]{1,0:T(8,128)(2,1)S(1)} fusion(f32[768,768]{1,0:T(8,128)S(1)} %fusion.3, bf16[768,4096]{1,0:T(8,128)(2,1)S(1)} %copy-done.1, bf16[1,4096,768]{2,1,0:T(8,128)(2,1)} %param.9), kind=kOutput, calls=%fused_computation.15 | convolution fusion | flops 4835377152 | bytes 16121856 | tf_op jit(solution)/shard_map/expert_ffn/dot_general | solution.py:21
  365.3 0.0 slice-done
  365.4 7.1 %convolution_convert_fusion.1 = bf16[768,4096]{1,0:T(8,128)(2,1)} fusion(bf16[768,768]{1,0:T(8,128)(2,1)S(1)} %multiply_convert_fusion, bf16[1,768,4096]{2,1,0:T(8,128)(2,1)S(1)} %bitcast.50), kind=kOutput, calls=%fused_computation.1 | convolution fusion | flops 4834983936 | bytes 13762560 | tf_op jit(solution)/shard_map/expert_ffn/dot_general | solution.py:23
  372.5 24.0 %all_to_all.17 = bf16[128,1,24576]{2,1,0:T(2,128)(2,1)} reshape(bf16[768,4096]{1,0:T(8,128)(2,1)} %convolution_convert_fusion.1) | data formatting | bytes 12582912 | tf_op jit(solution)/shard_map/return/all_to_all | solution.py:57
  396.5 38.8 %reduce.3 = bf16[128,24576]{1,0:T(8,128)(2,1)} reduce(bf16[128,1,24576]{2,1,0:T(2,128)(2,1)} %all_to_all.17, bf16[]{:T(256)} %broadcast.85), dimensions={1}, to_apply=%all_to_all.17.reduce_sub_computation | reduce | bytes 12582914 | tf_op jit(solution)/shard_map/return/all_to_all | solution.py:57
  435.3 9.4 %reshape.92 = bf16[128,2,12288]{2,1,0:T(2,128)(2,1)} reshape(bf16[128,24576]{1,0:T(8,128)(2,1)} %reduce.3) | data formatting | bytes 12582912
  444.7 8.5 %all-to-all-start.1 = ((bf16[128,2,12288]{2,1,0:T(2,128)(2,1)}), bf16[128,2,12288]{2,1,0:T(2,128)(2,1)}, u32[]{:S(2)}, u32[]{:S(2)}) async-start(bf16[128,2,12288]{2,1,0:T(2,128)(2,1)} %reshape.92), calls=%async_computation.1 | async-start | bytes 12582912 | tf_op jit(solution)/shard_map/return/all_to_all | solution.py:57
  453.2 0.1 copy.71
  453.3 0.8 select_reduce_fusion
  454.1 74.8 %all-to-all-done.1 = bf16[128,2,12288]{2,1,0:T(2,128)(2,1)} async-done(((bf16[128,2,12288]{2,1,0:T(2,128)(2,1)}), bf16[128,2,12288]{2,1,0:T(2,128)(2,1)}, u32[]{:S(2)}, u32[]{:S(2)}) %all-to-all-start.1) | async-done | bytes 6291488 | tf_op jit(solution)/shard_map/return/all_to_all | solution.py:57
  528.9 33.8 %reshape.93 = bf16[128,1,24576]{2,1,0:T(2,128)(2,1)} reshape(bf16[128,2,12288]{2,1,0:T(2,128)(2,1)} %all-to-all-done.1) | data formatting | bytes 12582912
  562.7 38.3 %reduce.1 = bf16[128,24576]{1,0:T(8,128)(2,1)} reduce(bf16[128,1,24576]{2,1,0:T(2,128)(2,1)} %reshape.93, bf16[]{:T(256)} %constant.43), dimensions={1}, to_apply=%all_to_all.15.reduce_sub_computation | reduce | bytes 12582914 | tf_op jit(solution)/shard_map/return/all_to_all | solution.py:57
  601.0 11.1 %reshape.87 = bf16[768,4096]{1,0:T(8,128)(2,1)} reshape(bf16[128,24576]{1,0:T(8,128)(2,1)} %reduce.1) | data formatting | bytes 12582912 | tf_op jit(solution)/shard_map/return/reshape | solution.py:60
  612.1 3.9 convolution_bitcast_fusion.1
  616.0 7.2 %fusion.7 = f32[96,4096]{1,0:T(8,128)S(1)} fusion(bf16[768,4096]{1,0:T(8,128)(2,1)} %get-tuple-element.5, bf16[96,4096]{1,0:T(8,128)(2,1)S(1)} %copy-done, bf16[4096,768]{1,0:T(8,128)(2,1)} %get-tuple-element.6, f32[96]{0:T(128)S(1)} %get-tuple-element.12, f32[96,768]{1,0:T(8,128)S(1)} %convolution_bitcast_fusion.1), kind=kOutput, calls=%fused_computation.14 | convolution fusion | flops 1209581568 | bytes 15237504 | tf_op jit(solution)/shard_map/hot_expert/dot_general | solution.py:23
  623.2 6.8 %fusion.5 = bf16[96,4096]{1,0:T(8,128)(2,1)} fusion(f32[96,4096]{1,0:T(8,128)S(1)} %fusion.7, f32[768,96]{0,1:T(8,128)S(1)} %select_reduce_fusion, bf16[768,4096]{1,0:T(8,128)(2,1)} %reshape.87), kind=kOutput, calls=%fused_computation.11 | convolution fusion | flops 3624665088 | bytes 8945664 | tf_op jit(solution)/shard_map/combine/dot_general | solution.py:66
  (14 shorter events, 0.1 us)
Async XLA Ops:
  6.5 90.5 %copy-start = (bf16[96,4096]{1,0:T(8,128)(2,1)S(1)}, bf16[96,4096]{1,0:T(8,128)(2,1)}, u32[]{:S(2)}) copy-start(bf16[96,4096]{1,0:T(8,128)(2,1)} %param.7) | copy-start | bytes 2359300
  6.5 88.9 %all-reduce.7.cloned.1.call-start = ((), (), s32[]{:S(2)}) async-start(), calls=%async_computation.3 | async-start | bytes 37748736 | tf_op jit(solution)/shard_map/hot_weight_broadcast/psum | solution.py:12
  23.1 0.7 copy-start.2
  23.2 588.9 %all-reduce.5.cloned.1.call-start = ((), (), s32[]{:S(2)}) async-start(), calls=%async_computation.2 | async-start | bytes 37748736 | tf_op jit(solution)/shard_map/hot_weight_broadcast/psum | solution.py:12
  336.3 29.1 %slice-start = ((s8[6291456]{0:T(1024)(128)(4,1)}), s8[2097152]{0:T(1024)(128)(4,1)S(1)}, s32[]{:S(2)}) async-start(s8[6291456]{0:T(1024)(128)(4,1)} %bitcast.49), calls=%async_computation.4 | async-start | bytes 4194304
  347.8 9.4 %copy-start.1 = (bf16[768,4096]{1,0:T(8,128)(2,1)S(1)}, bf16[768,4096]{1,0:T(8,128)(2,1)}, u32[]{:S(2)}) copy-start(bf16[768,4096]{1,0:T(8,128)(2,1)} %reshape.86) | copy-start | bytes 18874372
  347.8 17.6 %slice-start.1 = ((s8[6291456]{0:T(1024)(128)(4,1)}), s8[4194304]{0:T(1024)(128)(4,1)S(1)}, s32[]{:S(2)}) async-start(s8[6291456]{0:T(1024)(128)(4,1)} %bitcast.49), calls=%async_computation.5 | async-start | bytes 8388608
  444.7 8.5 %copy-start.3 = (f32[96,8]{0,1:T(8,128)S(1)}, f32[96,8]{0,1:T(8,128)}, u32[]{:S(2)}) copy-start(f32[96,8]{0,1:T(8,128)} %param.12) | copy-start | bytes 9220
  444.7 84.2 %all-to-all-start.1 = ((bf16[128,2,12288]{2,1,0:T(2,128)(2,1)}), bf16[128,2,12288]{2,1,0:T(2,128)(2,1)}, u32[]{:S(2)}, u32[]{:S(2)}) async-start(bf16[128,2,12288]{2,1,0:T(2,128)(2,1)} %reshape.92), calls=%async_computation.1 | async-start | bytes 12582912 | tf_op jit(solution)/shard_map/return/all_to_all | solution.py:57
Sparse Core Ops, SparseCore 0:
  23.3 72.0 all-reduce.6
  102.7 296.8 all-reduce.4
